TPU v7x, 256 devices: a whole 4x4x8 slice. The times are simulated.
256 devices in a mesh: row: 128 (over y, z, x), head: 2 (over core).
Axes of the slice: x: 4, y: 4, z: 8, core: 2. Of those that a mesh axis runs over, the one named last changes fastest.
Arguments:
- query_single: bfloat16 [128, 384], P('row'), may hold values from -6 to 6
- key_single: bfloat16 [8192, 384], P('row'), may hold values from -6 to 6
- pair: bfloat16 [128, 8192, 128], P('row'), may hold values from -6 to 32
- query_frames: float32 [12, 128], P(None, 'row'), may hold values from -2.5 to 2.5, as said below
- key_frames: float32 [12, 8192], P(None, 'row'), may hold values from -2.5 to 2.5, as said below
- w_query: bfloat16 [384, 96], P(None, 'head'), may hold values from -0.3125 to 0.3125
- w_key: bfloat16 [384, 96], P(None, 'head'), may hold values from -0.3125 to 0.3125
- w_value: bfloat16 [384, 96], P(None, 'head'), may hold values from -0.3125 to 0.3125
- w_query_points: bfloat16 [384, 72], P(None, 'head'), may hold values from -0.3125 to 0.3125
- w_key_points: bfloat16 [384, 72], P(None, 'head'), may hold values from -0.3125 to 0.3125
- w_value_points: bfloat16 [384, 144], P(None, 'head'), may hold values from -0.3125 to 0.3125
- head_weight: float32 [6], P('head'), may hold values from -2.5 to 0.5
- bias_weight: bfloat16 [6, 128], P('head'), as said below
- w_out: bfloat16 [1056, 384], P('head'), may hold values from -0.1875 to 0.1875
- d_out: bfloat16 [128, 384], P('row'), may hold values from -24 to 24
Outputs:
- output: bfloat16 [128, 384], P('row')
- grad_query: float32 [128, 384], P('row')
- grad_keys: float32 [8192, 384], P('row')
Inputs may be any that keep to these rules, and one draw needn't show every extreme that they name: `bias_weight`: entries within -2.5 and 2.5 over the square root of 128. `query_frames`: rows 0 to 8 of each column form a rotation matrix. `key_frames`: rows 0 to 8 of each column form a rotation matrix.
All inputs are finite; a program needn't handle non-finite values.
Results may differ from a plain program's by a relative error of at most 0.012.
The roundings to bfloat16 on the way count: a program that leaves them out, or rounds other values in their place, can miss the bound.
Values may be sent and summed in bfloat16 or wider, within the bound.
A program may use at most 64 MiB of HBM per device.

v0:
```python
import math
import jax
import jax.numpy as jnp
from jax import lax
from jax.sharding import PartitionSpec as P

C = 16
PQ = 4
PV = 8
LOGIT_SCALE = math.sqrt(1.0 / 3.0)


def point_scale(points):
    return math.sqrt(2.0 / (9.0 * points))


def product(form, former, latter):
    return jnp.einsum(form, former, latter, preferred_element_type=jnp.float32)


def frame_parts(frames):
    columns = frames.shape[1]
    return (frames[:9].reshape(3, 3, columns), frames[9:12])


def rotate(vectors, rotation):
    return jnp.einsum("xyn,nhpy->nhpx", rotation, vectors, precision=lax.Precision.HIGHEST)


def unrotate(vectors, rotation):
    return jnp.einsum("xyn,nhpx->nhpy", rotation, vectors, precision=lax.Precision.HIGHEST)


def split_columns(packed, extents, axis_index):
    pieces = []
    cursor = 0
    for extent in extents:
        pieces.append(lax.slice_in_dim(packed, cursor, cursor + extent, axis=axis_index))
        cursor = cursor + extent
    return pieces


def key_side(key_single, key_frames, w_key, w_value, w_key_points, w_value_points, head_count):
    rows_k = key_single.shape[0]
    rotation, offset = frame_parts(key_frames)
    offset_rows = jnp.transpose(offset)[:, None, None, :]
    keys_b = jnp.dot(key_single, w_key, preferred_element_type=jnp.float32).astype(jnp.bfloat16)
    values_b = jnp.dot(key_single, w_value, preferred_element_type=jnp.float32).astype(jnp.bfloat16)
    local_k = jnp.dot(key_single, w_key_points, preferred_element_type=jnp.float32).reshape(
        rows_k, head_count, PQ, 3
    )
    key_pts = (rotate(local_k, rotation) + offset_rows).astype(jnp.bfloat16).reshape(rows_k, -1)
    local_v = jnp.dot(key_single, w_value_points, preferred_element_type=jnp.float32).reshape(
        rows_k, head_count, PV, 3
    )
    value_pts = (rotate(local_v, rotation) + offset_rows).astype(jnp.bfloat16).reshape(rows_k, -1)
    return (keys_b, values_b, key_pts, value_pts)


def query_pass(
    query_single,
    pair,
    query_frames,
    w_query,
    w_query_points,
    head_weight,
    bias_weight,
    w_out,
    d_out,
    keys_all,
    values_all,
    kp_all,
    vp_all,
):
    rows_q = query_single.shape[0]
    head_count = head_weight.shape[0]
    rotation, offset = frame_parts(query_frames)
    offset_rows = jnp.transpose(offset)[:, None, None, :]
    point_gain = (jax.nn.softplus(head_weight) * point_scale(PQ))[None, :, None]
    query_b = (
        jnp.dot(query_single, w_query, preferred_element_type=jnp.float32)
        .astype(jnp.bfloat16)
        .reshape(rows_q, head_count, C)
    )
    local_q = jnp.dot(query_single, w_query_points, preferred_element_type=jnp.float32).reshape(
        rows_q, head_count, PQ, 3
    )
    query_pts = (
        (rotate(local_q, rotation) + offset_rows)
        .astype(jnp.bfloat16)
        .reshape(rows_q, head_count, 3 * PQ)
    )
    query_sq = jnp.sum(jnp.square(query_pts.astype(jnp.float32)), axis=-1)
    key_sq = jnp.sum(jnp.square(kp_all.astype(jnp.float32)), axis=-1)
    pair_bias = product("hc,qkc->qhk", bias_weight, pair)
    distance = (
        query_sq[:, :, None]
        + jnp.transpose(key_sq)[None, :, :]
        - 2.0 * product("qhe,khe->qhk", query_pts, kp_all)
    )
    logits = LOGIT_SCALE * (
        product("qhc,khc->qhk", query_b, keys_all) / math.sqrt(C)
        + pair_bias
        - 0.5 * point_gain * distance
    )
    attention = jax.nn.softmax(logits, axis=-1)
    attention_b = attention.astype(jnp.bfloat16)
    attended = product("qhk,khc->qhc", attention_b, values_all)
    point_sum = product("qhk,khe->qhe", attention_b, vp_all).reshape(rows_q, head_count, PV, 3)
    pair_out = product("qhk,qkc->qhc", attention_b, pair)
    local_pts = unrotate(point_sum - offset_rows, rotation)
    lengths = jnp.sqrt(1.0 + jnp.sum(jnp.square(local_pts), axis=-1))
    features = jnp.concatenate(
        [attended, local_pts.reshape(rows_q, head_count, 3 * PV), lengths, pair_out], axis=-1
    )
    features = features.astype(jnp.bfloat16).reshape(rows_q, -1)
    output_part = jnp.dot(features, w_out, preferred_element_type=jnp.float32)
    d_features = jnp.dot(d_out, jnp.transpose(w_out), preferred_element_type=jnp.float32).reshape(
        rows_q, head_count, -1
    )
    d_attended = d_features[:, :, :C].astype(jnp.bfloat16)
    d_local = d_features[:, :, C : C + 3 * PV].reshape(rows_q, head_count, PV, 3)
    d_lengths = d_features[:, :, C + 3 * PV : C + 4 * PV]
    d_pair = d_features[:, :, C + 4 * PV :].astype(jnp.bfloat16)
    d_local = d_local + (d_lengths / lengths)[..., None] * local_pts
    d_points = rotate(d_local, rotation).astype(jnp.bfloat16).reshape(rows_q, head_count, 3 * PV)
    d_attention = (
        product("qhc,khc->qhk", d_attended, values_all)
        + product("qhe,khe->qhk", d_points, vp_all)
        + product("qhc,qkc->qhk", d_pair, pair)
    )
    row_total = jnp.sum(attention * d_attention, axis=-1, keepdims=True)
    score_b = (LOGIT_SCALE * attention * (d_attention - row_total)).astype(jnp.bfloat16)
    d_query = product("qhk,khc->qhc", score_b, keys_all) / math.sqrt(C)
    score_rows = jnp.sum(score_b.astype(jnp.float32), axis=-1)[:, :, None]
    d_qpts = point_gain * (
        product("qhk,khe->qhe", score_b, kp_all) - score_rows * query_pts.astype(jnp.float32)
    )
    d_qlocal = (
        unrotate(d_qpts.reshape(rows_q, head_count, PQ, 3), rotation)
        .astype(jnp.bfloat16)
        .reshape(rows_q, -1)
    )
    grad_part = jnp.dot(
        d_query.astype(jnp.bfloat16).reshape(rows_q, -1),
        jnp.transpose(w_query),
        preferred_element_type=jnp.float32,
    )
    grad_part = grad_part + jnp.dot(
        d_qlocal, jnp.transpose(w_query_points), preferred_element_type=jnp.float32
    )
    query_side = jnp.concatenate(
        [
            query_b.reshape(rows_q, -1),
            query_pts.reshape(rows_q, -1),
            d_attended.reshape(rows_q, -1),
            d_points.reshape(rows_q, -1),
        ],
        axis=1,
    )
    return (output_part, grad_part, query_side, attention_b, score_b)


def key_terms(attention_b, score_b, query_side, key_points, point_gain, head_count):
    count_q = query_side.shape[0]
    count_k = key_points.shape[0]
    side_parts = split_columns(
        query_side, [head_count * C, head_count * 3 * PQ, head_count * C, head_count * 3 * PV], 1
    )
    query_b = side_parts[0].reshape(count_q, head_count, C)
    query_pts = side_parts[1].reshape(count_q, head_count, 3 * PQ)
    grad_att = side_parts[2].reshape(count_q, head_count, C)
    grad_pts = side_parts[3].reshape(count_q, head_count, 3 * PV)
    d_key = product("qhk,qhc->khc", score_b, query_b) / math.sqrt(C)
    score_sum = jnp.sum(score_b.astype(jnp.float32), axis=0)
    d_kpts = point_gain * (
        product("qhk,qhe->khe", score_b, query_pts)
        - jnp.transpose(score_sum)[:, :, None] * key_points.astype(jnp.float32)
    )
    d_value = product("qhk,qhc->khc", attention_b, grad_att)
    d_vpts = product("qhk,qhe->khe", attention_b, grad_pts)
    return jnp.concatenate(
        [
            d_key.reshape(count_k, -1),
            d_value.reshape(count_k, -1),
            d_kpts.reshape(count_k, -1),
            d_vpts.reshape(count_k, -1),
        ],
        axis=1,
    )


def key_finish(key_rows, key_frames, w_key, w_value, w_key_points, w_value_points, head_count):
    rows_k = key_rows.shape[0]
    rotation, offset = frame_parts(key_frames)
    pieces = split_columns(
        key_rows, [head_count * C, head_count * C, head_count * 3 * PQ, head_count * 3 * PV], 1
    )
    kp_local = (
        unrotate(pieces[2].reshape(rows_k, head_count, PQ, 3), rotation)
        .astype(jnp.bfloat16)
        .reshape(rows_k, -1)
    )
    vp_local = (
        unrotate(pieces[3].reshape(rows_k, head_count, PV, 3), rotation)
        .astype(jnp.bfloat16)
        .reshape(rows_k, -1)
    )
    result = jnp.dot(
        pieces[0].astype(jnp.bfloat16), jnp.transpose(w_key), preferred_element_type=jnp.float32
    )
    result = result + jnp.dot(
        pieces[1].astype(jnp.bfloat16), jnp.transpose(w_value), preferred_element_type=jnp.float32
    )
    result = result + jnp.dot(
        kp_local, jnp.transpose(w_key_points), preferred_element_type=jnp.float32
    )
    return result + jnp.dot(
        vp_local, jnp.transpose(w_value_points), preferred_element_type=jnp.float32
    )


def shards(
    query_single,
    key_single,
    pair,
    query_frames,
    key_frames,
    w_query,
    w_key,
    w_value,
    w_query_points,
    w_key_points,
    w_value_points,
    head_weight,
    bias_weight,
    w_out,
    d_out,
):
    head_count = head_weight.shape[0]
    keys_b, values_b, key_pts, value_pts = key_side(
        key_single, key_frames, w_key, w_value, w_key_points, w_value_points, head_count
    )
    packed = jnp.concatenate([keys_b, values_b, key_pts, value_pts], axis=1)
    gathered = lax.all_gather(packed, "row", axis=0, tiled=True)
    total_keys = gathered.shape[0]
    pieces = split_columns(
        gathered, [head_count * C, head_count * C, head_count * 3 * PQ, head_count * 3 * PV], 1
    )
    keys_all = pieces[0].reshape(total_keys, head_count, C)
    values_all = pieces[1].reshape(total_keys, head_count, C)
    kp_all = pieces[2].reshape(total_keys, head_count, 3 * PQ)
    vp_all = pieces[3].reshape(total_keys, head_count, 3 * PV)
    output_part, grad_part, query_side, attention_b, score_b = query_pass(
        query_single,
        pair,
        query_frames,
        w_query,
        w_query_points,
        head_weight,
        bias_weight,
        w_out,
        d_out,
        keys_all,
        values_all,
        kp_all,
        vp_all,
    )
    output = lax.psum(output_part, "head").astype(jnp.bfloat16)
    point_gain = (jax.nn.softplus(head_weight) * point_scale(PQ))[None, :, None]
    scores = jnp.concatenate([attention_b, score_b], axis=1)
    rows_n = lax.axis_size("row")
    local_k = key_single.shape[0]
    scores = scores.reshape(2 * head_count, rows_n, local_k)
    scores = lax.all_to_all(scores, "row", split_axis=1, concat_axis=1, tiled=True)
    scores = jnp.transpose(scores, (1, 0, 2))
    side_all = lax.all_gather(query_side, "row", axis=0, tiled=True)
    key_rows = key_terms(
        scores[:, :head_count],
        scores[:, head_count:],
        side_all,
        key_pts.reshape(local_k, head_count, 3 * PQ),
        point_gain,
        head_count,
    )
    grad_keys_part = key_finish(
        key_rows, key_frames, w_key, w_value, w_key_points, w_value_points, head_count
    )
    grad_query, grad_keys = lax.psum((grad_part, grad_keys_part), "head")
    return (output, grad_query, grad_keys)


def solution(mesh):
    return jax.shard_map(
        shards,
        mesh=mesh,
        in_specs=(
            P("row", None),
            P("row", None),
            P("row", None, None),
            P(None, "row"),
            P(None, "row"),
            P(None, "head"),
            P(None, "head"),
            P(None, "head"),
            P(None, "head"),
            P(None, "head"),
            P(None, "head"),
            P("head"),
            P("head", None),
            P("head", None),
            P("row", None),
        ),
        out_specs=(P("row", None), P("row", None), P("row", None)),
        check_vma=False,
    )
```

profile of v0, /device:TPU:1, one launch (start us, length us, event | category | flops | bytes accessed | tf_op | source)
XLA Modules:
  0.0 621.8 jit_solution(9938110551300458424)
XLA Ops:
  7.2 0.8 slice_bitcast_fusion
  8.9 0.9 fusion.64
  10.2 7.5 %fusion.65 = f32[64,3,4,3]{2,3,1,0:T(4,128)S(1)} fusion(f32[64,3,4,3]{3,2,1,0:T(4,128)S(1)} %copy.139, f32[3,3,64,1]{0,1,3,2:T(4,128)S(1)} %copy.198), kind=kOutput, calls=%fused_computation.113 | convolution fusion | flops 82944 | bytes 20736 | tf_op jit(solution)/shard_map/xyn,nhpy->nhpx/dot_general | solution.py:27
  18.4 1.1 fusion.7
  19.7 0.9 convolution_convert_fusion.3
  20.6 0.9 convolution_convert_fusion.4
  22.7 0.8 reshape.333
  26.3 0.9 fusion.18
  31.2 108.1 %all-gather.3.cloned.1.call-done = bf16[8192,204]{1,0:T(8,128)(2,1)} async-done(((bf16[64,204]{1,0:T(8,128)(2,1)}), bf16[8192,204]{1,0:T(8,128)(2,1)}) %all-gather.3.cloned.1.call-update) | async-done | bytes 3342352 | tf_op jit(solution)/shard_map/all_gather | solution.py:245
  139.3 4.2 slice.77
  143.5 2.9 copy.151
  146.5 1.2 reshape.335
  147.7 1.0 multiply_reduce_fusion
  149.0 4.9 fusion.59
  153.8 2.7 copy.211
  156.5 1.4 fusion.67
  157.9 1.7 fusion.63
  160.6 3.6 slice.78
  164.2 3.8 copy.212
  167.9 1.7 fusion.29
  171.0 1.6 fusion.61
  172.6 0.7 fusion.41
  173.4 1.4 convolution_convert_fusion.6
  174.8 1.4 copy.158
  176.2 1.3 reshape.404
  177.5 1.3 reshape_reshape.14
  178.8 0.8 maximum_bitcast_fusion
  179.6 304.1 %all-gather = bf16[128,1,204]{2,1,0:T(2,128)(2,1)} all-gather(bf16[1,1,204]{2,1,0:T(2,128)(2,1)S(1)} %maximum_bitcast_fusion), channel_id=1, replica_groups=mesh['row'=128,'head'=2] {'row'}, dimensions={0}, use_global_device_ids=true | all-gather | bytes 52632 | tf_op jit(solution)/shard_map/all_gather | solution.py:277
  483.6 1.6 copy.163
  485.3 1.3 slice.88
  486.6 1.3 slice.87
  487.9 2.2 fusion.70
  490.1 2.6 copy.210
  492.8 1.4 fusion.50
  494.2 1.8 fusion.20
  496.0 0.8 convert_reduce_fusion
  496.8 1.0 fusion.25
  499.4 0.9 reshape.419
  500.3 6.1 all-to-all-start
  508.2 0.8 fusion.60
  509.0 8.4 %all-to-all-done = bf16[128,2,192]{2,1,0:T(2,128)(2,1)S(1)} async-done(((bf16[128,2,192]{2,1,0:T(2,128)(2,1)}), bf16[128,2,192]{2,1,0:T(2,128)(2,1)S(1)}, u32[]{:S(2)}, u32[]{:S(2)}) %all-to-all-start) | async-done | bytes 98336 | tf_op jit(solution)/shard_map/all_to_all | solution.py:275
  517.8 0.9 convolution_bitcast_fusion.1
  519.0 1.0 convolution_convert_fusion
  520.6 7.4 %convolution_convert_fusion.1 = bf16[64,3,4,3]{2,3,1,0:T(4,128)(2,1)S(1)} fusion(f32[64,3,4,3]{3,2,1,0:T(4,128)S(1)} %copy.169, f32[3,3,64,1]{0,1,3,2:T(4,128)S(1)} %copy.198), kind=kOutput, calls=%fused_computation.12 | convolution fusion | flops 85248 | bytes 16128 | tf_op jit(solution)/shard_map/xyn,nhpx->nhpy/dot_general | solution.py:31
  529.1 0.8 convolution_add_fusion.2
  530.2 65.1 %all-reduce = (bf16[1,384]{1,0:T(2,128)(2,1)}, f32[1,384]{1,0:T(1,128)}) all-reduce(f32[1,384]{1,0:T(1,128)S(1)} %fusion.69, f32[1,384]{1,0:T(1,128)S(1)} %add.116), channel_id=1, replica_groups=mesh['row'=128,'head'=2] {'head'}, use_global_device_ids=true, to_apply=%region_5.6 | all-reduce | flops 768 | bytes 5376 | tf_op jit(solution)/shard_map/psum | solution.py:269
  595.2 18.1 %all-reduce.3.cloned.1.call-done = f32[64,384]{1,0:T(8,128)} async-done(((f32[64,384]{1,0:T(8,128)}), f32[64,384]{1,0:T(8,128)}) %all-reduce.3.cloned.1.call-update) | async-done | bytes 98320 | tf_op jit(solution)/shard_map/psum | solution.py:289
  613.4 1.5 copy.242
  (153 shorter events, 18.5 us)
Async XLA Ops:
  7.2 150.7 %copy-start = (bf16[1,8192,128]{2,1,0:T(8,128)(2,1)S(1)}, bf16[1,8192,128]{2,1,0:T(8,128)(2,1)}, u32[]{:S(2)}) copy-start(bf16[1,8192,128]{2,1,0:T(8,128)(2,1)} %param.17) | copy-start | bytes 6291460
  7.2 10.8 %copy-start.4 = (bf16[64,384]{1,0:T(8,128)(2,1)S(1)}, bf16[64,384]{1,0:T(8,128)(2,1)}, u32[]{:S(2)}) copy-start(bf16[64,384]{1,0:T(8,128)(2,1)} %param.16) | copy-start | bytes 147460
  7.2 10.8 %copy-start.6 = (bf16[384,72]{0,1:T(8,128)(2,1)S(1)}, bf16[384,72]{0,1:T(8,128)(2,1)}, u32[]{:S(2)}) copy-start(bf16[384,72]{0,1:T(8,128)(2,1)} %param.25) | copy-start | bytes 165892
  7.2 132.1 %all-gather.3.cloned.1.call-start = ((), (), s32[]{:S(2)}) async-start(), calls=%async_computation.1 | async-start | bytes 4227072 | tf_op jit(solution)/shard_map/all_gather | solution.py:245
  8.8 13.5 %copy-start.3 = (bf16[528,384]{1,0:T(8,128)(2,1)S(1)}, bf16[528,384]{1,0:T(8,128)(2,1)}, u32[]{:S(2)}) copy-start(bf16[528,384]{1,0:T(8,128)(2,1)} %param.28) | copy-start | bytes 1216516
  8.8 13.5 %copy-start.25 = (bf16[1,384]{1,0:T(2,128)(2,1)S(1)}, bf16[1,384]{1,0:T(2,128)(2,1)}, u32[]{:S(2)}) copy-start(bf16[1,384]{1,0:T(2,128)(2,1)} %param.29) | copy-start | bytes 2308
  9.9 12.7 %copy-start.29 = (f32[12,1]{0,1:T(1,128)S(1)}, f32[12,1]{0,1:T(1,128)}, u32[]{:S(2)}) copy-start(f32[12,1]{0,1:T(1,128)} %param.18) | copy-start | bytes 148
  10.1 13.4 %copy-start.28 = (bf16[1,384]{1,0:T(2,128)(2,1)S(1)}, bf16[1,384]{1,0:T(2,128)(2,1)}, u32[]{:S(2)}) copy-start(bf16[1,384]{1,0:T(2,128)(2,1)} %param.15) | copy-start | bytes 2308
  10.1 20.5 %copy-start.30 = (f32[3]{0:T(128)S(1)}, f32[3]{0:T(128)}, u32[]{:S(2)}) copy-start(f32[3]{0:T(128)} %param.26) | copy-start | bytes 40
  22.5 121.0 %copy-start.16 = (f32[1,3,176]{2,1,0:T(4,128)}, f32[1,3,176]{2,1,0:T(4,128)S(1)}, u32[]{:S(2)}) copy-start(f32[1,3,176]{2,1,0:T(4,128)S(1)} %copy.189) | copy-start | bytes 6340
  22.6 121.0 %copy-start.18 = (bf16[1,3,176]{2,1,0:T(4,128)(2,1)}, bf16[1,3,176]{2,1,0:T(4,128)(2,1)S(1)}, u32[]{:S(2)}) copy-start(bf16[1,3,176]{2,1,0:T(4,128)(2,1)S(1)} %copy.237) | copy-start | bytes 3172
  22.7 4.6 copy-start.19
  27.2 116.3 %copy-start.24 = (bf16[48]{0:T(256)(128)(2,1)}, bf16[48]{0:T(256)(128)(2,1)S(1)}, u32[]{:S(2)}) copy-start(bf16[48]{0:T(256)(128)(2,1)S(1)} %fusion.18) | copy-start | bytes 292
  153.8 4.1 copy-start.27
  492.8 4.0 copy-start.5
  494.2 3.6 copy-start.1
  496.0 2.2 copy-start.2
  498.6 8.1 %copy-start.13 = (bf16[128,36]{0,1:T(8,128)(2,1)S(1)}, bf16[128,36]{0,1:T(8,128)(2,1)}, u32[]{:S(2)}) copy-start(bf16[128,36]{0,1:T(8,128)(2,1)} %slice.87) | copy-start | bytes 27652
  498.6 8.1 %copy-start.20 = (bf16[3,12]{1,0:T(4,128)(2,1)S(1)}, bf16[3,12]{1,0:T(4,128)(2,1)}, u32[]{:S(2)}) copy-start(bf16[3,12]{1,0:T(4,128)(2,1)} %reshape.336) | copy-start | bytes 220
  498.6 8.1 %copy-start.21 = (f32[3]{0:T(128)S(1)}, f32[3]{0:T(128)}, u32[]{:S(2)}) copy-start(f32[3]{0:T(128)} %get-tuple-element.5) | copy-start | bytes 40
  498.6 8.1 %copy-start.23 = (f32[3]{0:T(128)S(1)}, f32[3]{0:T(128)}, u32[]{:S(2)}) copy-start(f32[3]{0:T(128)} %get-tuple-element.7) | copy-start | bytes 40
  498.6 8.1 %copy-start.26 = (f32[3,1,12]{2,1,0:T(1,128)S(1)}, f32[3,1,12]{2,1,0:T(1,128)}, u32[]{:S(2)}) copy-start(f32[3,1,12]{2,1,0:T(1,128)} %fusion.25) | copy-start | bytes 436
  498.6 8.3 %copy-start.15 = (f32[3,3]{1,0:T(4,128)S(1)}, f32[3,3]{1,0:T(4,128)}, u32[]{:S(2)}) copy-start(f32[3,3]{1,0:T(4,128)} %reshape.334) | copy-start | bytes 112
  498.6 8.9 %copy-start.14 = (bf16[384,48]{0,1:T(8,128)(2,1)S(1)}, bf16[384,48]{0,1:T(8,128)(2,1)}, u32[]{:S(2)}) copy-start(bf16[384,48]{0,1:T(8,128)(2,1)} %param.20) | copy-start | bytes 110596
  498.6 9.0 %copy-start.17 = (bf16[3,8,3]{1,2,0:T(4,128)(2,1)S(1)}, bf16[3,8,3]{1,2,0:T(4,128)(2,1)}, u32[]{:S(2)}) copy-start(bf16[3,8,3]{1,2,0:T(4,128)(2,1)} %get-tuple-element.15) | copy-start | bytes 436
  499.2 20.9 %copy-start.12 = (f32[64,3,4,3]{0,1,3,2:T(4,128)S(1)}, f32[64,3,4,3]{0,1,3,2:T(4,128)}, u32[]{:S(2)}) copy-start(f32[64,3,4,3]{0,1,3,2:T(4,128)} %copy.166) | copy-start | bytes 27652
  499.2 20.9 %copy-start.22 = (f32[3]{0:T(128)S(1)}, f32[3]{0:T(128)}, u32[]{:S(2)}) copy-start(f32[3]{0:T(128)} %get-tuple-element.5) | copy-start | bytes 40
  500.3 17.1 %all-to-all-start = ((bf16[128,2,192]{2,1,0:T(2,128)(2,1)}), bf16[128,2,192]{2,1,0:T(2,128)(2,1)S(1)}, u32[]{:S(2)}, u32[]{:S(2)}) async-start(bf16[128,2,192]{2,1,0:T(2,128)(2,1)} %reshape.419), calls=%async_computation | async-start | bytes 262144 | tf_op jit(solution)/shard_map/all_to_all | solution.py:275
  506.4 107.0 %all-reduce.3.cloned.1.call-start = ((), (), s32[]{:S(2)}) async-start(), calls=%async_computation.2 | async-start | bytes 196608 | tf_op jit(solution)/shard_map/psum | solution.py:289
  508.2 20.3 %copy-start.8 = (bf16[384,48]{0,1:T(8,128)(2,1)S(1)}, bf16[384,48]{0,1:T(8,128)(2,1)}, u32[]{:S(2)}) copy-start(bf16[384,48]{0,1:T(8,128)(2,1)} %param.21) | copy-start | bytes 110596
  509.0 19.7 %copy-start.9 = (bf16[384,48]{0,1:T(8,128)(2,1)S(1)}, bf16[384,48]{0,1:T(8,128)(2,1)}, u32[]{:S(2)}) copy-start(bf16[384,48]{0,1:T(8,128)(2,1)} %param.22) | copy-start | bytes 110596
  517.5 11.4 %copy-start.11 = (bf16[384,36]{0,1:T(8,128)(2,1)S(1)}, bf16[384,36]{0,1:T(8,128)(2,1)}, u32[]{:S(2)}) copy-start(bf16[384,36]{0,1:T(8,128)(2,1)} %param.24) | copy-start | bytes 82948
  517.5 11.6 %copy-start.7 = (bf16[384,72]{0,1:T(8,128)(2,1)S(1)}, bf16[384,72]{0,1:T(8,128)(2,1)}, u32[]{:S(2)}) copy-start(bf16[384,72]{0,1:T(8,128)(2,1)} %param.25) | copy-start | bytes 165892
  518.7 11.3 %copy-start.10 = (bf16[384,36]{0,1:T(8,128)(2,1)S(1)}, bf16[384,36]{0,1:T(8,128)(2,1)}, u32[]{:S(2)}) copy-start(bf16[384,36]{0,1:T(8,128)(2,1)} %param.23) | copy-start | bytes 82948
Sparse Core Ops, SparseCore 0:
  22.4 116.8 all-gather.2
  530.1 83.2 all-reduce.2
where the time goes:
time: 623 us; the launch traced here: 622 us
  blocking collectives  369 us (59%)
  waiting for transfers between devices  135 us (22%)
  local copies, waits for them, and re-layouts  50.5 us (8%)
  matrix products  40.5 us (7%)
  between operations  14.7 us (2%)
  starting transfers between devices  6.41 us (1%)
    all_gather x1, blocking collectives, shards(): side_all = lax.all_gather(query_side, 'row', axis=0, tiled=True)  304 us
    all_gather x1, waiting for transfers between devices, shards(): gathered = lax.all_gather(packed, 'row', axis=0, tiled=True)  108 us
    psum x1, blocking collectives, shards(): output = lax.psum(output_part, 'head').astype(jnp.bfloat16)  65.1 us
    slice x7, local copies, waits for them, and re-layouts, split_columns(): lax.slice_in_dim(packed, cursor, cursor + extent, axis=axis_index)  19 us
    psum x1, waiting for transfers between devices, shards(): grad_query, grad_keys = lax.psum((grad_part, grad_keys_part), 'head')  18.1 us
    dot_general x15, matrix products, product(): return jnp.einsum(form, former, latter, preferred_element_type=jnp.float32)  13.8 us
  transfers between devices with their start and end apart: 3, of which 3 were waited for; matrix products, arithmetic and copies ran while one was open for 2% of the time, Pallas kernels for 0%

commit v1 on v0

--- a/solution.py
+++ b/solution.py
@@ -266,7 +266,7 @@
         kp_all,
         vp_all,
     )
-    output = lax.psum(output_part, "head").astype(jnp.bfloat16)
+    output = jnp.sum(lax.all_gather(output_part, "head"), axis=0).astype(jnp.bfloat16)
     point_gain = (jax.nn.softplus(head_weight) * point_scale(PQ))[None, :, None]
     scores = jnp.concatenate([attention_b, score_b], axis=1)
     rows_n = lax.axis_size("row")

time: 623 us -> 625 us (level)
    all_gather x0 -> x1, blocking collectives: none -> 62.2 us  [shards(): lax.all_gather(output_part, 'head')]
    psum x1, blocking collectives: 65.1 us -> 3.01 us  [shards(): grad_query, grad_keys = lax.psum((grad_part, grad_keys_part), 'head')]
where the time goes in v1:
time: 625 us; the launch traced here: 623 us
  blocking collectives  370 us (59%)
  waiting for transfers between devices  132 us (21%)
  local copies, waits for them, and re-layouts  52.9 us (8%)
  matrix products  42 us (7%)
  between operations  14.6 us (2%)
  starting transfers between devices  6.46 us (1%)
    all_gather x1, blocking collectives, shards(): side_all = lax.all_gather(query_side, 'row', axis=0, tiled=True)  305 us
    all_gather x1, waiting for transfers between devices, shards(): gathered = lax.all_gather(packed, 'row', axis=0, tiled=True)  108 us
    all_gather x1, blocking collectives, shards(): lax.all_gather(output_part, 'head')  62.2 us
    slice x7, local copies, waits for them, and re-layouts, split_columns(): lax.slice_in_dim(packed, cursor, cursor + extent, axis=axis_index)  19.6 us
    psum x1, waiting for transfers between devices, shards(): grad_query, grad_keys = lax.psum((grad_part, grad_keys_part), 'head')  16.7 us
    dot_general x15, matrix products, product(): return jnp.einsum(form, former, latter, preferred_element_type=jnp.float32)  15.2 us
  transfers between devices with their start and end apart: 3, of which 3 were waited for; matrix products, arithmetic and copies ran while one was open for 2% of the time, Pallas kernels for 0%

profile of v1, /device:TPU:1, one launch (start us, length us, event | category | flops | bytes accessed | tf_op | source)
XLA Modules:
  0.0 623.2 jit_solution(12716236129625980748)
XLA Ops:
  7.2 0.8 slice_bitcast_fusion
  8.9 0.9 fusion.64
  10.2 7.5 %fusion.65 = f32[64,3,4,3]{2,3,1,0:T(4,128)S(1)} fusion(f32[64,3,4,3]{3,2,1,0:T(4,128)S(1)} %copy.139, f32[3,3,64,1]{0,1,3,2:T(4,128)S(1)} %copy.198), kind=kOutput, calls=%fused_computation.114 | convolution fusion | flops 82944 | bytes 20736 | tf_op jit(solution)/shard_map/xyn,nhpy->nhpx/dot_general | solution.py:27
  18.4 1.1 fusion.7
  19.7 0.9 convolution_convert_fusion.3
  20.6 0.9 convolution_convert_fusion.4
  22.7 0.8 reshape.344
  26.3 0.9 fusion.18
  31.2 108.1 %all-gather.5.cloned.1.call-done = bf16[8192,204]{1,0:T(8,128)(2,1)} async-done(((bf16[64,204]{1,0:T(8,128)(2,1)}), bf16[8192,204]{1,0:T(8,128)(2,1)}) %all-gather.5.cloned.1.call-update) | async-done | bytes 3342352 | tf_op jit(solution)/shard_map/all_gather | solution.py:245
  139.3 4.2 slice.77
  143.5 3.0 copy.151
  146.5 1.2 reshape.346
  147.7 1.0 multiply_reduce_fusion
  149.0 4.9 fusion.59
  153.9 2.7 copy.211
  156.6 1.4 fusion.67
  158.0 1.7 fusion.63
  160.7 3.6 slice.78
  164.3 3.8 copy.212
  168.1 1.7 fusion.29
  171.1 1.6 fusion.61
  173.5 1.4 convolution_convert_fusion.6
  174.9 1.4 copy.158
  176.3 1.3 reshape.420
  177.6 1.4 reshape_reshape.14
  179.8 304.5 %all-gather.2 = bf16[128,1,204]{2,1,0:T(2,128)(2,1)} all-gather(bf16[1,1,204]{2,1,0:T(2,128)(2,1)S(1)} %maximum_bitcast_fusion), channel_id=1, replica_groups=mesh['row'=128,'head'=2] {'row'}, dimensions={0}, use_global_device_ids=true | all-gather | bytes 52632 | tf_op jit(solution)/shard_map/all_gather | solution.py:277
  484.3 1.6 copy.163
  486.0 1.3 slice.88
  487.3 1.3 slice.87
  488.6 2.2 fusion.69
  490.8 2.6 copy.210
  493.4 1.4 fusion.50
  494.9 1.8 fusion.20
  497.5 1.0 fusion.25
  500.1 0.9 reshape.435
  501.0 6.2 all-to-all-start
  510.0 1.3 fusion.60
  511.4 6.7 %all-to-all-done = bf16[128,2,192]{2,1,0:T(2,128)(2,1)S(1)} async-done(((bf16[128,2,192]{2,1,0:T(2,128)(2,1)}), bf16[128,2,192]{2,1,0:T(2,128)(2,1)S(1)}, u32[]{:S(2)}, u32[]{:S(2)}) %all-to-all-start) | async-done | bytes 98336 | tf_op jit(solution)/shard_map/all_to_all | solution.py:275
  518.6 0.9 convolution_bitcast_fusion.1
  519.7 1.0 convolution_convert_fusion
  520.9 0.8 fusion.9
  522.0 7.4 %convolution_convert_fusion.1 = bf16[64,3,4,3]{2,3,1,0:T(4,128)(2,1)S(1)} fusion(f32[64,3,4,3]{3,2,1,0:T(4,128)S(1)} %copy.169, f32[3,3,64,1]{0,1,3,2:T(4,128)S(1)} %copy.198), kind=kOutput, calls=%fused_computation.12 | convolution fusion | flops 85248 | bytes 16128 | tf_op jit(solution)/shard_map/xyn,nhpx->nhpy/dot_general | solution.py:31
  529.8 0.9 fusion.10
  531.3 0.8 convolution_add_fusion.2
  532.3 62.2 %all-gather.1 = f32[2,1,384]{2,1,0:T(1,128)S(1)} all-gather(f32[1,1,384]{2,1,0:T(1,128)S(1)} %convolution_bitcast_fusion.3), channel_id=2, replica_groups=mesh['row'=128,'head'=2] {'head'}, dimensions={0}, use_global_device_ids=true | all-gather | bytes 4608 | tf_op jit(solution)/shard_map/all_gather | solution.py:269
  595.0 3.0 psum.14
  598.0 16.7 %all-reduce.2.cloned.1.call-done = f32[64,384]{1,0:T(8,128)} async-done(((f32[64,384]{1,0:T(8,128)}), f32[64,384]{1,0:T(8,128)}) %all-reduce.2.cloned.1.call-update) | async-done | bytes 98320 | tf_op jit(solution)/shard_map/psum | solution.py:289
  614.8 1.5 copy.242
  (156 shorter events, 22.3 us)
Async XLA Ops:
  7.2 150.8 %copy-start = (bf16[1,8192,128]{2,1,0:T(8,128)(2,1)S(1)}, bf16[1,8192,128]{2,1,0:T(8,128)(2,1)}, u32[]{:S(2)}) copy-start(bf16[1,8192,128]{2,1,0:T(8,128)(2,1)} %param.17) | copy-start | bytes 6291460
  7.2 10.8 %copy-start.4 = (bf16[64,384]{1,0:T(8,128)(2,1)S(1)}, bf16[64,384]{1,0:T(8,128)(2,1)}, u32[]{:S(2)}) copy-start(bf16[64,384]{1,0:T(8,128)(2,1)} %param.16) | copy-start | bytes 147460
  7.2 10.8 %copy-start.6 = (bf16[384,72]{0,1:T(8,128)(2,1)S(1)}, bf16[384,72]{0,1:T(8,128)(2,1)}, u32[]{:S(2)}) copy-start(bf16[384,72]{0,1:T(8,128)(2,1)} %param.25) | copy-start | bytes 165892
  7.2 132.1 %all-gather.5.cloned.1.call-start = ((), (), s32[]{:S(2)}) async-start(), calls=%async_computation.1 | async-start | bytes 4227072 | tf_op jit(solution)/shard_map/all_gather | solution.py:245
  8.8 13.5 %copy-start.3 = (bf16[528,384]{1,0:T(8,128)(2,1)S(1)}, bf16[528,384]{1,0:T(8,128)(2,1)}, u32[]{:S(2)}) copy-start(bf16[528,384]{1,0:T(8,128)(2,1)} %param.28) | copy-start | bytes 1216516
  8.8 13.5 %copy-start.25 = (bf16[1,384]{1,0:T(2,128)(2,1)S(1)}, bf16[1,384]{1,0:T(2,128)(2,1)}, u32[]{:S(2)}) copy-start(bf16[1,384]{1,0:T(2,128)(2,1)} %param.29) | copy-start | bytes 2308
  9.9 12.7 %copy-start.29 = (f32[12,1]{0,1:T(1,128)S(1)}, f32[12,1]{0,1:T(1,128)}, u32[]{:S(2)}) copy-start(f32[12,1]{0,1:T(1,128)} %param.18) | copy-start | bytes 148
  10.1 13.4 %copy-start.28 = (bf16[1,384]{1,0:T(2,128)(2,1)S(1)}, bf16[1,384]{1,0:T(2,128)(2,1)}, u32[]{:S(2)}) copy-start(bf16[1,384]{1,0:T(2,128)(2,1)} %param.15) | copy-start | bytes 2308
  10.1 20.5 %copy-start.30 = (f32[3]{0:T(128)S(1)}, f32[3]{0:T(128)}, u32[]{:S(2)}) copy-start(f32[3]{0:T(128)} %param.26) | copy-start | bytes 40
  22.5 121.0 %copy-start.16 = (f32[1,3,176]{2,1,0:T(4,128)}, f32[1,3,176]{2,1,0:T(4,128)S(1)}, u32[]{:S(2)}) copy-start(f32[1,3,176]{2,1,0:T(4,128)S(1)} %copy.189) | copy-start | bytes 6340
  22.6 121.0 %copy-start.18 = (bf16[1,3,176]{2,1,0:T(4,128)(2,1)}, bf16[1,3,176]{2,1,0:T(4,128)(2,1)S(1)}, u32[]{:S(2)}) copy-start(bf16[1,3,176]{2,1,0:T(4,128)(2,1)S(1)} %copy.237) | copy-start | bytes 3172
  22.7 4.5 copy-start.19
  27.2 116.3 %copy-start.24 = (bf16[48]{0:T(256)(128)(2,1)}, bf16[48]{0:T(256)(128)(2,1)S(1)}, u32[]{:S(2)}) copy-start(bf16[48]{0:T(256)(128)(2,1)S(1)} %fusion.18) | copy-start | bytes 292
  153.9 4.1 copy-start.27
  493.4 4.0 copy-start.5
  494.9 3.6 copy-start.1
  496.6 2.2 copy-start.2
  499.2 8.1 %copy-start.13 = (bf16[128,36]{0,1:T(8,128)(2,1)S(1)}, bf16[128,36]{0,1:T(8,128)(2,1)}, u32[]{:S(2)}) copy-start(bf16[128,36]{0,1:T(8,128)(2,1)} %slice.87) | copy-start | bytes 27652
  499.2 8.8 %copy-start.21 = (bf16[3,12]{1,0:T(4,128)(2,1)S(1)}, bf16[3,12]{1,0:T(4,128)(2,1)}, u32[]{:S(2)}) copy-start(bf16[3,12]{1,0:T(4,128)(2,1)} %reshape.347) | copy-start | bytes 220
  499.2 8.8 %copy-start.22 = (f32[3]{0:T(128)S(1)}, f32[3]{0:T(128)}, u32[]{:S(2)}) copy-start(f32[3]{0:T(128)} %get-tuple-element.3) | copy-start | bytes 40
  499.3 8.8 %copy-start.23 = (f32[3]{0:T(128)S(1)}, f32[3]{0:T(128)}, u32[]{:S(2)}) copy-start(f32[3]{0:T(128)} %get-tuple-element.5) | copy-start | bytes 40
  499.3 8.7 %copy-start.26 = (f32[3,1,12]{2,1,0:T(1,128)S(1)}, f32[3,1,12]{2,1,0:T(1,128)}, u32[]{:S(2)}) copy-start(f32[3,1,12]{2,1,0:T(1,128)} %fusion.25) | copy-start | bytes 436
  499.3 8.9 %copy-start.15 = (f32[3,3]{1,0:T(4,128)S(1)}, f32[3,3]{1,0:T(4,128)}, u32[]{:S(2)}) copy-start(f32[3,3]{1,0:T(4,128)} %reshape.345) | copy-start | bytes 112
  499.3 9.4 %copy-start.10 = (bf16[384,36]{0,1:T(8,128)(2,1)S(1)}, bf16[384,36]{0,1:T(8,128)(2,1)}, u32[]{:S(2)}) copy-start(bf16[384,36]{0,1:T(8,128)(2,1)} %param.23) | copy-start | bytes 82948
  499.3 9.6 %copy-start.14 = (bf16[384,48]{0,1:T(8,128)(2,1)S(1)}, bf16[384,48]{0,1:T(8,128)(2,1)}, u32[]{:S(2)}) copy-start(bf16[384,48]{0,1:T(8,128)(2,1)} %param.20) | copy-start | bytes 110596
  499.3 10.3 %copy-start.17 = (bf16[3,8,3]{1,2,0:T(4,128)(2,1)S(1)}, bf16[3,8,3]{1,2,0:T(4,128)(2,1)}, u32[]{:S(2)}) copy-start(bf16[3,8,3]{1,2,0:T(4,128)(2,1)} %get-tuple-element.13) | copy-start | bytes 436
  501.0 17.1 %all-to-all-start = ((bf16[128,2,192]{2,1,0:T(2,128)(2,1)}), bf16[128,2,192]{2,1,0:T(2,128)(2,1)S(1)}, u32[]{:S(2)}, u32[]{:S(2)}) async-start(bf16[128,2,192]{2,1,0:T(2,128)(2,1)} %reshape.435), calls=%async_computation | async-start | bytes 262144 | tf_op jit(solution)/shard_map/all_to_all | solution.py:275
  507.1 107.7 %all-reduce.2.cloned.1.call-start = ((), (), s32[]{:S(2)}) async-start(), calls=%async_computation.2 | async-start | bytes 196608 | tf_op jit(solution)/shard_map/psum | solution.py:289
  509.8 20.9 %copy-start.8 = (bf16[384,48]{0,1:T(8,128)(2,1)S(1)}, bf16[384,48]{0,1:T(8,128)(2,1)}, u32[]{:S(2)}) copy-start(bf16[384,48]{0,1:T(8,128)(2,1)} %param.21) | copy-start | bytes 110596
  511.4 19.5 %copy-start.9 = (bf16[384,48]{0,1:T(8,128)(2,1)S(1)}, bf16[384,48]{0,1:T(8,128)(2,1)}, u32[]{:S(2)}) copy-start(bf16[384,48]{0,1:T(8,128)(2,1)} %param.22) | copy-start | bytes 110596
  518.2 12.8 %copy-start.11 = (bf16[384,36]{0,1:T(8,128)(2,1)S(1)}, bf16[384,36]{0,1:T(8,128)(2,1)}, u32[]{:S(2)}) copy-start(bf16[384,36]{0,1:T(8,128)(2,1)} %param.24) | copy-start | bytes 82948
  518.3 13.0 %copy-start.7 = (bf16[384,72]{0,1:T(8,128)(2,1)S(1)}, bf16[384,72]{0,1:T(8,128)(2,1)}, u32[]{:S(2)}) copy-start(bf16[384,72]{0,1:T(8,128)(2,1)} %param.25) | copy-start | bytes 165892
  518.4 11.2 %copy-start.12 = (bf16[128,48]{0,1:T(8,128)(2,1)S(1)}, bf16[128,48]{0,1:T(8,128)(2,1)}, u32[]{:S(2)}) copy-start(bf16[128,48]{0,1:T(8,128)(2,1)} %get-tuple-element.11) | copy-start | bytes 36868
  519.7 75.4 %copy-start.20 = (f32[1,384]{1,0:T(1,128)S(1)}, f32[1,384]{1,0:T(1,128)}, u32[]{:S(2)}) copy-start(f32[1,384]{1,0:T(1,128)} %add.114) | copy-start | bytes 4612
Sparse Core Ops, SparseCore 0:
  22.4 116.8 all-gather.4
  532.3 82.4 all-reduce.1
